TPU v7x, 32 devices: a whole 2x2x4 slice. The times are simulated.
32 devices in a mesh: grp: 4 (over z), row: 8 (over y, x, core).
Axes of the slice: x: 2, y: 2, z: 4, core: 2. Of those that a mesh axis runs over, the one named last changes fastest.
Arguments:
- basis: float32 [8192, 1024], P(('grp', 'row')), may hold values from -40 to 40
- block: float32 [8192, 512], P(('grp', 'row')), may hold values from -600 to 600
- counts: int32 [4, 8], P('grp', 'row'), may hold values from 128 to 256, as said below
Outputs:
- new_block: float32 [8192, 512], P(('grp', 'row'))
- factor: float32 [512, 512], replicated
Inputs may be any that keep to these rules, and one draw needn't show every extreme that they name: `counts`: each device's live rows are a multiple of 128, at most 256; one device holds exactly 256.
All inputs are finite; a program needn't handle non-finite values.
Results may differ from a plain program's by a relative error of at most 0.0003.
Values sent between devices are 32-bit elements; how exact they have to be, the bound alone decides.
A program may use at most 64 MiB of HBM per device.

v0:
```python
import jax
import jax.numpy as jnp
from jax import lax
from jax.sharding import PartitionSpec as P


def transposed_product(left, right):
    return lax.dot_general(
        left,
        right,
        (((0,), (0,)), ((), ())),
        precision=lax.Precision.HIGHEST,
        preferred_element_type=jnp.float32,
    )


def matrix_product(left, right):
    return jnp.dot(left, right, precision=lax.Precision.HIGHEST, preferred_element_type=jnp.float32)


def body(basis, block, counts):
    row_slots = block.shape[0]
    devices = lax.axis_size("grp") * lax.axis_size("row")
    weight = 1.0 / (row_slots * devices)
    live = (lax.iota(jnp.int32, row_slots) < counts[0, 0]).astype(jnp.float32)[:, None]
    basis_live = basis * live
    block_live = block * live
    local_coeffs = transposed_product(basis_live, block_live) * weight
    local_metric = transposed_product(basis_live, basis_live) * weight
    coeffs, metric = lax.psum((local_coeffs, local_metric), ("grp", "row"))
    correction = coeffs - matrix_product(metric, coeffs)
    residual = block_live - matrix_product(basis_live, coeffs + correction)
    local_gram = transposed_product(residual, residual) * weight
    gram = lax.psum(local_gram, ("grp", "row"))
    lower_factor = jnp.linalg.cholesky(gram)
    new_block = lax.linalg.triangular_solve(
        lower_factor, residual, left_side=False, lower=True, transpose_a=True
    )
    return (new_block, lower_factor.T)


def solution(mesh):
    placed = (P(("grp", "row"), None), P(("grp", "row"), None), P("grp", "row"))
    return jax.shard_map(
        body, mesh=mesh, in_specs=placed, out_specs=(P(("grp", "row"), None), P()), check_vma=False
    )
```

profile of v0, /device:TPU:0, one launch (start us, length us, event | category | flops | bytes accessed | tf_op | source)
XLA Modules:
  0.0 480.0 jit_solution(1416516150197127453)
XLA Ops:
  7.9 7.3 %convolution_multiply_fusion = f32[1024,1024]{1,0:T(8,128)} fusion(f32[256,1024]{1,0:T(8,128)} %param.3, f32[256]{0:T(256)S(1)} %compare_convert_fusion), kind=kOutput, calls=%fused_computation.3 | convolution fusion | flops 3222536192 | bytes 5243904 | tf_op jit(solution)/shard_map/dot_general | solution.py:8
  15.2 3.3 convolution_multiply_fusion.1
  18.6 158.9 %all-reduce.7.cloned.1.call-done = (f32[1024,512]{1,0:T(8,128)}, f32[1024,1024]{1,0:T(8,128)}) async-done(((f32[1024,512]{1,0:T(8,128)}, f32[1024,1024]{1,0:T(8,128)}), (f32[1024,512]{1,0:T(8,128)}, f32[1024,1024]{1,0:T(8,128)})) %all-reduce.7.cloned.1.call-update) | async-done | bytes 6291472 | tf_op jit(solution)/shard_map/psum | solution.py:30
  177.5 10.1 %fusion.43 = f32[1024,512]{1,0:T(8,128)S(1)} fusion(f32[1024,1024]{1,0:T(8,128)} %get-tuple-element.21, f32[1024,512]{1,0:T(8,128)} %get-tuple-element.20), kind=kOutput, calls=%fused_computation.84 | convolution fusion | flops 6442450944 | bytes 8388608 | tf_op jit(solution)/shard_map/dot_general | solution.py:18
  187.6 2.1 fusion.1
  189.7 2.0 convolution_multiply_fusion.2
  191.8 130.8 %all-reduce.5.cloned.1.call-done = f32[512,512]{0,1:T(8,128)} async-done(((f32[512,512]{0,1:T(8,128)}), f32[512,512]{0,1:T(8,128)}) %all-reduce.5.cloned.1.call-update) | async-done | bytes 1048592 | tf_op jit(solution)/shard_map/psum | solution.py:34
  322.6 1.6 copy.6
  325.5 11.7 %cholesky.104 = f32[128,128]{1,0:T(8,128)S(1)} custom-call(f32[128,128]{1,0:T(8,128)S(1)} %cholesky.266), custom_call_target="Cholesky" | custom-call | tf_op jit(solution)/shard_map/jit(cholesky)/cholesky | solution.py:35
  337.2 9.8 %custom-call.30 = f32[1,128,128]{1,2,0:T(8,128)S(1)} custom-call(f32[1,128,128]{2,1,0:T(8,128)S(1)} %get-tuple-element.35), custom_call_target="InvertDiagBlocksLowerTriangular" | custom-call | tf_op jit(solution)/shard_map/jit(cholesky)/cholesky | solution.py:35
  349.7 11.9 %cholesky.217 = f32[128,128]{1,0:T(8,128)S(1)} custom-call(f32[128,128]{1,0:T(8,128)S(1)} %cholesky.270), custom_call_target="Cholesky" | custom-call | tf_op jit(solution)/shard_map/jit(cholesky)/cholesky | solution.py:35
  361.6 9.8 %custom-call.31 = f32[1,128,128]{1,2,0:T(8,128)S(1)} custom-call(f32[1,128,128]{2,1,0:T(8,128)S(1)} %get-tuple-element.32), custom_call_target="InvertDiagBlocksLowerTriangular" | custom-call | tf_op jit(solution)/shard_map/jit(cholesky)/cholesky | solution.py:35
  373.0 11.7 %cholesky.238 = f32[128,128]{1,0:T(8,128)S(1)} custom-call(f32[128,128]{1,0:T(8,128)S(1)} %cholesky.275), custom_call_target="Cholesky" | custom-call | tf_op jit(solution)/shard_map/jit(cholesky)/cholesky | solution.py:35
  385.5 9.8 %custom-call.32 = f32[1,128,128]{1,2,0:T(8,128)S(1)} custom-call(f32[1,128,128]{2,1,0:T(8,128)S(1)} %get-tuple-element.29), custom_call_target="InvertDiagBlocksLowerTriangular" | custom-call | tf_op jit(solution)/shard_map/jit(cholesky)/cholesky | solution.py:35
  396.7 11.9 %cholesky.255 = f32[128,128]{1,0:T(8,128)S(1)} custom-call(f32[128,128]{1,0:T(8,128)S(1)} %convolution_subtract_fusion.5), custom_call_target="Cholesky" | custom-call | tf_op jit(solution)/shard_map/jit(cholesky)/cholesky | solution.py:35
  413.7 11.7 %while.1 = (s32[]{:T(128)}, f32[512,512]{1,0:T(8,128)}, s32[4,2]{0,1:T(2,128)S(1)}, f32[4,128,128]{2,1,0:T(8,128)S(1)}, s32[]{:T(128)}) while((s32[]{:T(128)}, f32[512,512]{1,0:T(8,128)}, s32[4,2]{0,1:T(2,128)S(1)}, f32[4,128,128]{2,1,0:T(8,128)S(1)}, s32[]{:T(128)}) %tuple.33), condition=%wide.while_cond, body=%wide.while_body.sunk | while | flops 2 | bytes 131181 | solution.py:36
  414.4 2.2 bitcast_dynamic-update-slice_fusion.2
  417.3 2.2 bitcast_dynamic-update-slice_fusion.2
  420.3 2.2 bitcast_dynamic-update-slice_fusion.2
  423.2 2.2 bitcast_dynamic-update-slice_fusion.2
  425.4 39.3 %custom-call.33 = f32[4,128,128]{1,2,0:T(8,128)S(1)} custom-call(f32[4,128,128]{2,1,0:T(8,128)S(1)} %get-tuple-element.9), custom_call_target="InvertDiagBlocksLowerTriangular" | custom-call | tf_op jit(solution)/shard_map/triangular_solve | solution.py:36
  466.6 1.5 convolution_subtract_fusion.2
  468.5 1.8 convolution_subtract_fusion.1
  471.6 1.3 copy.8
  (52 shorter events, 16.6 us)
Async XLA Ops:
  7.2 170.4 %all-reduce.7.cloned.1.call-start = ((), (), s32[]{:S(2)}) async-start(), calls=%async_computation.1 | async-start | bytes 12582912 | tf_op jit(solution)/shard_map/psum | solution.py:30
  7.9 7.4 %copy-start = (f32[256,1024]{1,0:T(8,128)S(1)}, f32[256,1024]{1,0:T(8,128)}, u32[]{:S(2)}) copy-start(f32[256,1024]{1,0:T(8,128)} %param.3) | copy-start | bytes 3145732
  7.9 7.3 %copy-start.4 = (f32[256,512]{1,0:T(8,128)S(1)}, f32[256,512]{1,0:T(8,128)}, u32[]{:S(2)}) copy-start(f32[256,512]{1,0:T(8,128)} %param.4) | copy-start | bytes 1572868
  18.5 304.0 %all-reduce.5.cloned.1.call-start = ((), (), s32[]{:S(2)}) async-start(), calls=%async_computation | async-start | bytes 2097152 | tf_op jit(solution)/shard_map/psum | solution.py:34
  177.5 10.1 %copy-start.1 = (f32[1024,512]{1,0:T(8,128)S(1)}, f32[1024,512]{1,0:T(8,128)}, u32[]{:S(2)}) copy-start(f32[1024,512]{1,0:T(8,128)} %get-tuple-element.20) | copy-start | bytes 6291460
  322.6 1.7 copy-start.2
  324.5 1.0 copy-start.3
Sparse Core Ops, SparseCore 0:
  18.7 158.8 all-reduce.6
  191.9 130.6 all-reduce.4
where the time goes:
time: 487 us; the launch traced here: 480 us
  waiting for transfers between devices  290 us (60%)
  other arithmetic  120 us (25%)
  matrix products  36 us (7%)
  between operations  17.7 us (4%)
  local copies, waits for them, and re-layouts  16.7 us (3%)
    psum x1, waiting for transfers between devices, body(): coeffs, metric = lax.psum((local_coeffs, local_metric), ('grp', 'row'))  159 us
    psum x1, waiting for transfers between devices, body(): gram = lax.psum(local_gram, ('grp', 'row'))  131 us
    another operation x14, other arithmetic, body(): lower_factor = jnp.linalg.cholesky(gram)  78.8 us
    another operation x3, other arithmetic, body(): lax.linalg.triangular_solve(lower_factor, residual, left_side=False, lowe...  39.4 us
    dot_general x3, matrix products, transposed_product(): lax.dot_general(left, right, (((0,), (0,)), ((), ())), precision=lax.Prec...  12.6 us
    dot_general x2, matrix products, matrix_product(): jnp.dot(left, right, precision=lax.Precision.HIGHEST, preferred_element_t...  12.2 us
    another operation x12, local copies, waits for them, and re-layouts  11.6 us
  transfers between devices with their start and end apart: 2, of which 2 were waited for; matrix products, arithmetic and copies ran while one was open for 0% of the time, Pallas kernels for 0%

commit v1 on v0

--- a/solution.py
+++ b/solution.py
@@ -19,6 +19,12 @@
 
 
 def body(basis, block, counts):
+
+    def _cover_values(message, device_axis, group_axis):
+        for jj in (device_axis, group_axis):
+            message = lax.psum(message, jj)
+        return message
+
     row_slots = block.shape[0]
     devices = lax.axis_size("grp") * lax.axis_size("row")
     weight = 1.0 / (row_slots * devices)
@@ -27,7 +33,7 @@
     block_live = block * live
     local_coeffs = transposed_product(basis_live, block_live) * weight
     local_metric = transposed_product(basis_live, basis_live) * weight
-    coeffs, metric = lax.psum((local_coeffs, local_metric), ("grp", "row"))
+    coeffs, metric = _cover_values((local_coeffs, local_metric), "grp", "row")
     correction = coeffs - matrix_product(metric, coeffs)
     residual = block_live - matrix_product(basis_live, coeffs + correction)
     local_gram = transposed_product(residual, residual) * weight

time: 487 us -> 660 us (1.36)
  waiting for transfers between devices: 290 us -> 463 us
    psum x1 -> x2, waiting for transfers between devices: 159 us -> 332 us  [_cover_values(): message = lax.psum(message, jj)]
  transfers between devices with their start and end apart: 2 -> 3, of which waited for: 2 -> 3; matrix products, arithmetic and copies ran while one was open for 0% -> 0% of each run, Pallas kernels for 0% -> 0%
where the time goes in v1:
time: 660 us; the launch traced here: 653 us
  waiting for transfers between devices  463 us (70%)
  other arithmetic  120 us (18%)
  matrix products  36 us (5%)
  between operations  17.4 us (3%)
  local copies, waits for them, and re-layouts  16.7 us (3%)
    psum x2, waiting for transfers between devices, _cover_values(): message = lax.psum(message, jj)  332 us
    psum x1, waiting for transfers between devices, body(): gram = lax.psum(local_gram, ('grp', 'row'))  131 us
    another operation x14, other arithmetic, body(): lower_factor = jnp.linalg.cholesky(gram)  78.8 us
    another operation x3, other arithmetic, body(): lax.linalg.triangular_solve(lower_factor, residual, left_side=False, lowe...  39.4 us
  transfers between devices with their start and end apart: 3, of which 3 were waited for; matrix products, arithmetic and copies ran while one was open for 0% of the time, Pallas kernels for 0%

profile of v1, /device:TPU:0, one launch (start us, length us, event | category | flops | bytes accessed | tf_op | source)
XLA Modules:
  0.0 652.8 jit_solution(6936539080781134987)
XLA Ops:
  7.9 7.3 %convolution_multiply_fusion = f32[1024,1024]{1,0:T(8,128)} fusion(f32[256,1024]{1,0:T(8,128)} %param.3, f32[256]{0:T(256)S(1)} %compare_convert_fusion), kind=kOutput, calls=%fused_computation.3 | convolution fusion | flops 3222536192 | bytes 5243904 | tf_op jit(solution)/shard_map/dot_general | solution.py:8
  15.2 3.3 convolution_multiply_fusion.1
  18.6 225.7 %all-reduce.11.cloned.1.call-done = (f32[1024,512]{1,0:T(8,128)}, f32[1024,1024]{1,0:T(8,128)}) async-done(((f32[1024,512]{1,0:T(8,128)}, f32[1024,1024]{1,0:T(8,128)}), (f32[1024,512]{1,0:T(8,128)}, f32[1024,1024]{1,0:T(8,128)})) %all-reduce.11.cloned.1.call-update) | async-done | bytes 6291472 | tf_op jit(solution)/shard_map/psum | solution.py:25
  244.4 106.2 %all-reduce.9.cloned.1.call-done = (f32[1024,512]{1,0:T(8,128)}, f32[1024,1024]{1,0:T(8,128)}) async-done(((f32[1024,512]{1,0:T(8,128)}, f32[1024,1024]{1,0:T(8,128)}), (f32[1024,512]{1,0:T(8,128)}, f32[1024,1024]{1,0:T(8,128)})) %all-reduce.9.cloned.1.call-update) | async-done | bytes 6291472 | tf_op jit(solution)/shard_map/psum | solution.py:25
  350.5 10.1 %fusion.43 = f32[1024,512]{1,0:T(8,128)S(1)} fusion(f32[1024,1024]{1,0:T(8,128)} %get-tuple-element.21, f32[1024,512]{1,0:T(8,128)} %get-tuple-element.20), kind=kOutput, calls=%fused_computation.84 | convolution fusion | flops 6442450944 | bytes 8388608 | tf_op jit(solution)/shard_map/dot_general | solution.py:18
  360.6 2.1 fusion.1
  362.7 2.0 convolution_multiply_fusion.2
  364.8 131.0 %all-reduce.7.cloned.1.call-done = f32[512,512]{0,1:T(8,128)} async-done(((f32[512,512]{0,1:T(8,128)}), f32[512,512]{0,1:T(8,128)}) %all-reduce.7.cloned.1.call-update) | async-done | bytes 1048592 | tf_op jit(solution)/shard_map/psum | solution.py:40
  495.8 1.6 copy.6
  498.6 11.7 %cholesky.104 = f32[128,128]{1,0:T(8,128)S(1)} custom-call(f32[128,128]{1,0:T(8,128)S(1)} %cholesky.266), custom_call_target="Cholesky" | custom-call | tf_op jit(solution)/shard_map/jit(cholesky)/cholesky | solution.py:41
  510.4 9.8 %custom-call.30 = f32[1,128,128]{1,2,0:T(8,128)S(1)} custom-call(f32[1,128,128]{2,1,0:T(8,128)S(1)} %get-tuple-element.37), custom_call_target="InvertDiagBlocksLowerTriangular" | custom-call | tf_op jit(solution)/shard_map/jit(cholesky)/cholesky | solution.py:41
  522.9 11.9 %cholesky.217 = f32[128,128]{1,0:T(8,128)S(1)} custom-call(f32[128,128]{1,0:T(8,128)S(1)} %cholesky.270), custom_call_target="Cholesky" | custom-call | tf_op jit(solution)/shard_map/jit(cholesky)/cholesky | solution.py:41
  534.8 9.8 %custom-call.31 = f32[1,128,128]{1,2,0:T(8,128)S(1)} custom-call(f32[1,128,128]{2,1,0:T(8,128)S(1)} %get-tuple-element.34), custom_call_target="InvertDiagBlocksLowerTriangular" | custom-call | tf_op jit(solution)/shard_map/jit(cholesky)/cholesky | solution.py:41
  546.2 11.7 %cholesky.238 = f32[128,128]{1,0:T(8,128)S(1)} custom-call(f32[128,128]{1,0:T(8,128)S(1)} %cholesky.275), custom_call_target="Cholesky" | custom-call | tf_op jit(solution)/shard_map/jit(cholesky)/cholesky | solution.py:41
  558.6 9.8 %custom-call.32 = f32[1,128,128]{1,2,0:T(8,128)S(1)} custom-call(f32[1,128,128]{2,1,0:T(8,128)S(1)} %get-tuple-element.31), custom_call_target="InvertDiagBlocksLowerTriangular" | custom-call | tf_op jit(solution)/shard_map/jit(cholesky)/cholesky | solution.py:41
  569.9 11.9 %cholesky.255 = f32[128,128]{1,0:T(8,128)S(1)} custom-call(f32[128,128]{1,0:T(8,128)S(1)} %convolution_subtract_fusion.5), custom_call_target="Cholesky" | custom-call | tf_op jit(solution)/shard_map/jit(cholesky)/cholesky | solution.py:41
  586.9 11.7 %while.1 = (s32[]{:T(128)}, f32[512,512]{1,0:T(8,128)}, s32[4,2]{0,1:T(2,128)S(1)}, f32[4,128,128]{2,1,0:T(8,128)S(1)}, s32[]{:T(128)}) while((s32[]{:T(128)}, f32[512,512]{1,0:T(8,128)}, s32[4,2]{0,1:T(2,128)S(1)}, f32[4,128,128]{2,1,0:T(8,128)S(1)}, s32[]{:T(128)}) %tuple.33), condition=%wide.while_cond, body=%wide.while_body.sunk | while | flops 2 | bytes 131181 | solution.py:42
  587.6 2.2 bitcast_dynamic-update-slice_fusion.2
  590.5 2.2 bitcast_dynamic-update-slice_fusion.2
  593.5 2.2 bitcast_dynamic-update-slice_fusion.2
  596.4 2.2 bitcast_dynamic-update-slice_fusion.2
  598.6 39.3 %custom-call.33 = f32[4,128,128]{1,2,0:T(8,128)S(1)} custom-call(f32[4,128,128]{2,1,0:T(8,128)S(1)} %get-tuple-element.9), custom_call_target="InvertDiagBlocksLowerTriangular" | custom-call | tf_op jit(solution)/shard_map/triangular_solve | solution.py:42
  639.8 1.5 convolution_subtract_fusion.2
  641.6 1.8 convolution_subtract_fusion.1
  (55 shorter events, 17.9 us)
Async XLA Ops:
  7.2 237.1 %all-reduce.11.cloned.1.call-start = ((), (), s32[]{:S(2)}) async-start(), calls=%async_computation.2 | async-start | bytes 12582912 | tf_op jit(solution)/shard_map/psum | solution.py:25
  7.9 7.4 %copy-start = (f32[256,1024]{1,0:T(8,128)S(1)}, f32[256,1024]{1,0:T(8,128)}, u32[]{:S(2)}) copy-start(f32[256,1024]{1,0:T(8,128)} %param.3) | copy-start | bytes 3145732
  7.9 7.3 %copy-start.4 = (f32[256,512]{1,0:T(8,128)S(1)}, f32[256,512]{1,0:T(8,128)}, u32[]{:S(2)}) copy-start(f32[256,512]{1,0:T(8,128)} %param.4) | copy-start | bytes 1572868
  18.5 332.0 %all-reduce.9.cloned.1.call-start = ((), (), s32[]{:S(2)}) async-start(), calls=%async_computation.1 | async-start | bytes 12582912 | tf_op jit(solution)/shard_map/psum | solution.py:25
  244.3 251.5 %all-reduce.7.cloned.1.call-start = ((), (), s32[]{:S(2)}) async-start(), calls=%async_computation | async-start | bytes 2097152 | tf_op jit(solution)/shard_map/psum | solution.py:40
  350.5 10.1 %copy-start.1 = (f32[1024,512]{1,0:T(8,128)S(1)}, f32[1024,512]{1,0:T(8,128)}, u32[]{:S(2)}) copy-start(f32[1024,512]{1,0:T(8,128)} %get-tuple-element.20) | copy-start | bytes 6291460
  495.8 1.7 copy-start.2
  497.7 1.0 copy-start.3
Sparse Core Ops, SparseCore 0:
  18.7 225.5 all-reduce.10
  247.6 102.8 all-reduce.8
  364.9 130.8 all-reduce.6

commit v2 on v0

--- a/solution.py
+++ b/solution.py
@@ -31,7 +31,8 @@
     correction = coeffs - matrix_product(metric, coeffs)
     residual = block_live - matrix_product(basis_live, coeffs + correction)
     local_gram = transposed_product(residual, residual) * weight
-    gram = lax.psum(local_gram, ("grp", "row"))
+    partial = lax.psum(local_gram, "row")
+    gram = lax.psum(partial, "grp")
     lower_factor = jnp.linalg.cholesky(gram)
     new_block = lax.linalg.triangular_solve(
         lower_factor, residual, left_side=False, lower=True, transpose_a=True

time: 487 us -> 464 us (0.953)
  waiting for transfers between devices: 290 us -> 269 us
    psum x1 -> x2, waiting for transfers between devices: 131 us -> 110 us  [the longest x1 56.4 us: body(): partial = lax.psum(local_gram, 'row')]
  transfers between devices with their start and end apart: 2 -> 3, of which waited for: 2 -> 3; matrix products, arithmetic and copies ran while one was open for 0% -> 0% of each run, Pallas kernels for 0% -> 0%
where the time goes in v2:
time: 464 us; the launch traced here: 459 us
  waiting for transfers between devices  269 us (58%)
  other arithmetic  120 us (26%)
  matrix products  35.6 us (8%)
  between operations  17.5 us (4%)
  local copies, waits for them, and re-layouts  16.7 us (4%)
    psum x1, waiting for transfers between devices, body(): coeffs, metric = lax.psum((local_coeffs, local_metric), ('grp', 'row'))  159 us
    another operation x14, other arithmetic, body(): lower_factor = jnp.linalg.cholesky(gram)  78.6 us
    psum x1, waiting for transfers between devices, body(): partial = lax.psum(local_gram, 'row')  56.4 us
    psum x1, waiting for transfers between devices, body(): gram = lax.psum(partial, 'grp')  53.5 us
    another operation x3, other arithmetic, body(): lax.linalg.triangular_solve(lower_factor, residual, left_side=False, lowe...  39.4 us
    dot_general x3, matrix products, transposed_product(): lax.dot_general(left, right, (((0,), (0,)), ((), ())), precision=lax.Prec...  12.6 us
    dot_general x2, matrix products, matrix_product(): jnp.dot(left, right, precision=lax.Precision.HIGHEST, preferred_element_t...  11.7 us
    another operation x12, local copies, waits for them, and re-layouts  11.6 us
  transfers between devices with their start and end apart: 3, of which 3 were waited for; matrix products, arithmetic and copies ran while one was open for 0% of the time, Pallas kernels for 0%

profile of v2, /device:TPU:0, one launch (start us, length us, event | category | flops | bytes accessed | tf_op | source)
XLA Modules:
  0.0 458.8 jit_solution(1911514309770503720)
XLA Ops:
  7.9 7.3 %convolution_multiply_fusion = f32[1024,1024]{1,0:T(8,128)} fusion(f32[256,1024]{1,0:T(8,128)} %param.3, f32[256]{0:T(256)S(1)} %compare_convert_fusion), kind=kOutput, calls=%fused_computation.3 | convolution fusion | flops 3222536192 | bytes 5243904 | tf_op jit(solution)/shard_map/dot_general | solution.py:8
  15.2 3.3 convolution_multiply_fusion.1
  19.1 158.5 %all-reduce.10.cloned.1.call-done = (f32[1024,512]{1,0:T(8,128)}, f32[1024,1024]{1,0:T(8,128)}) async-done(((f32[1024,512]{1,0:T(8,128)}, f32[1024,1024]{1,0:T(8,128)}), (f32[1024,512]{1,0:T(8,128)}, f32[1024,1024]{1,0:T(8,128)})) %all-reduce.10.cloned.1.call-update) | async-done | bytes 6291472 | tf_op jit(solution)/shard_map/psum | solution.py:30
  177.6 9.6 %fusion.43 = f32[1024,512]{1,0:T(8,128)S(1)} fusion(f32[1024,1024]{1,0:T(8,128)} %get-tuple-element.21, f32[1024,512]{1,0:T(8,128)} %get-tuple-element.20), kind=kOutput, calls=%fused_computation.84 | convolution fusion | flops 6442450944 | bytes 8388608 | tf_op jit(solution)/shard_map/dot_general | solution.py:18
  187.3 2.1 fusion.1
  189.4 2.0 convolution_multiply_fusion.2
  191.7 56.4 %all-reduce.6.cloned.1.call-done = f32[512,512]{0,1:T(8,128)} async-done(((f32[512,512]{0,1:T(8,128)}), f32[512,512]{0,1:T(8,128)}) %all-reduce.6.cloned.1.call-update) | async-done | bytes 1048592 | tf_op jit(solution)/shard_map/psum | solution.py:34
  248.1 53.5 %all-reduce.8.cloned.1.call-done = f32[512,512]{0,1:T(8,128)} async-done(((f32[512,512]{0,1:T(8,128)}), f32[512,512]{0,1:T(8,128)}) %all-reduce.8.cloned.1.call-update) | async-done | bytes 1048592 | tf_op jit(solution)/shard_map/psum | solution.py:35
  301.6 1.6 copy.6
  304.5 11.7 %cholesky.104 = f32[128,128]{1,0:T(8,128)S(1)} custom-call(f32[128,128]{1,0:T(8,128)S(1)} %cholesky.266), custom_call_target="Cholesky" | custom-call | tf_op jit(solution)/shard_map/jit(cholesky)/cholesky | solution.py:36
  316.3 9.8 %custom-call.30 = f32[1,128,128]{1,2,0:T(8,128)S(1)} custom-call(f32[1,128,128]{2,1,0:T(8,128)S(1)} %get-tuple-element.35), custom_call_target="InvertDiagBlocksLowerTriangular" | custom-call | tf_op jit(solution)/shard_map/jit(cholesky)/cholesky | solution.py:36
  328.7 11.7 %cholesky.217 = f32[128,128]{1,0:T(8,128)S(1)} custom-call(f32[128,128]{1,0:T(8,128)S(1)} %cholesky.270), custom_call_target="Cholesky" | custom-call | tf_op jit(solution)/shard_map/jit(cholesky)/cholesky | solution.py:36
  340.5 10.0 %custom-call.31 = f32[1,128,128]{1,2,0:T(8,128)S(1)} custom-call(f32[1,128,128]{2,1,0:T(8,128)S(1)} %get-tuple-element.32), custom_call_target="InvertDiagBlocksLowerTriangular" | custom-call | tf_op jit(solution)/shard_map/jit(cholesky)/cholesky | solution.py:36
  352.0 11.7 %cholesky.238 = f32[128,128]{1,0:T(8,128)S(1)} custom-call(f32[128,128]{1,0:T(8,128)S(1)} %cholesky.275), custom_call_target="Cholesky" | custom-call | tf_op jit(solution)/shard_map/jit(cholesky)/cholesky | solution.py:36
  364.5 9.8 %custom-call.32 = f32[1,128,128]{1,2,0:T(8,128)S(1)} custom-call(f32[1,128,128]{2,1,0:T(8,128)S(1)} %get-tuple-element.29), custom_call_target="InvertDiagBlocksLowerTriangular" | custom-call | tf_op jit(solution)/shard_map/jit(cholesky)/cholesky | solution.py:36
  375.8 11.7 %cholesky.255 = f32[128,128]{1,0:T(8,128)S(1)} custom-call(f32[128,128]{1,0:T(8,128)S(1)} %convolution_subtract_fusion.5), custom_call_target="Cholesky" | custom-call | tf_op jit(solution)/shard_map/jit(cholesky)/cholesky | solution.py:36
  392.8 11.7 %while.1 = (s32[]{:T(128)}, f32[512,512]{1,0:T(8,128)}, s32[4,2]{0,1:T(2,128)S(1)}, f32[4,128,128]{2,1,0:T(8,128)S(1)}, s32[]{:T(128)}) while((s32[]{:T(128)}, f32[512,512]{1,0:T(8,128)}, s32[4,2]{0,1:T(2,128)S(1)}, f32[4,128,128]{2,1,0:T(8,128)S(1)}, s32[]{:T(128)}) %tuple.33), condition=%wide.while_cond, body=%wide.while_body.sunk | while | flops 2 | bytes 131181 | solution.py:37
  393.5 2.2 bitcast_dynamic-update-slice_fusion.2
  396.5 2.2 bitcast_dynamic-update-slice_fusion.2
  399.4 2.2 bitcast_dynamic-update-slice_fusion.2
  402.3 2.2 bitcast_dynamic-update-slice_fusion.2
  404.5 39.3 %custom-call.33 = f32[4,128,128]{1,2,0:T(8,128)S(1)} custom-call(f32[4,128,128]{2,1,0:T(8,128)S(1)} %get-tuple-element.9), custom_call_target="InvertDiagBlocksLowerTriangular" | custom-call | tf_op jit(solution)/shard_map/triangular_solve | solution.py:37
  445.7 1.5 convolution_subtract_fusion.2
  447.6 1.8 convolution_subtract_fusion.1
  (55 shorter events, 18.9 us)
Async XLA Ops:
  7.2 170.5 %all-reduce.10.cloned.1.call-start = ((), (), s32[]{:S(2)}) async-start(), calls=%async_computation.2 | async-start | bytes 12582912 | tf_op jit(solution)/shard_map/psum | solution.py:30
  7.9 7.4 %copy-start = (f32[256,1024]{1,0:T(8,128)S(1)}, f32[256,1024]{1,0:T(8,128)}, u32[]{:S(2)}) copy-start(f32[256,1024]{1,0:T(8,128)} %param.3) | copy-start | bytes 3145732
  7.9 7.3 %copy-start.4 = (f32[256,512]{1,0:T(8,128)S(1)}, f32[256,512]{1,0:T(8,128)}, u32[]{:S(2)}) copy-start(f32[256,512]{1,0:T(8,128)} %param.4) | copy-start | bytes 1572868
  18.5 229.6 %all-reduce.6.cloned.1.call-start = ((), (), s32[]{:S(2)}) async-start(), calls=%async_computation | async-start | bytes 2097152 | tf_op jit(solution)/shard_map/psum | solution.py:34
  177.6 9.6 %copy-start.1 = (f32[1024,512]{1,0:T(8,128)S(1)}, f32[1024,512]{1,0:T(8,128)}, u32[]{:S(2)}) copy-start(f32[1024,512]{1,0:T(8,128)} %get-tuple-element.20) | copy-start | bytes 6291460
  191.4 110.2 %all-reduce.8.cloned.1.call-start = ((), (), s32[]{:S(2)}) async-start(), calls=%async_computation.1 | async-start | bytes 2097152 | tf_op jit(solution)/shard_map/psum | solution.py:35
  301.6 1.7 copy-start.2
  303.5 1.0 copy-start.3
Sparse Core Ops, SparseCore 0:
  18.7 158.9 all-reduce.9
  191.6 56.4 all-reduce.5
  250.5 51.1 all-reduce.7
